TPU v7x, 32 devices: a whole 2x2x4 slice. The times are simulated.
32 devices in a mesh: dp: 2 (over x), slot: 4 (over y, core), hid: 4 (over z).
Axes of the slice: x: 2, y: 2, z: 4, core: 2. Of those that a mesh axis runs over, the one named last changes fastest.
Arguments:
- master_weights: float32 [8, 3, 768, 2048], P('slot', None, 'hid', 'dp'), may hold values from -0.125 to 0.125
- first_moment: float32 [8, 3, 768, 2048], P('slot', None, 'hid', 'dp'), may hold values from -6 to 6
- second_moment: float32 [8, 3, 768, 2048], P('slot', None, 'hid', 'dp'), may hold values from 1 to 100
- tokens_one: bfloat16 [2048, 2048], P('dp'), may hold values from -6 to 6
- grad_out: bfloat16 [2048, 2048], P('dp'), may hold values from -6 to 6
- route_one: int32 [2048, 2], P('dp'), may hold values from 0 to 7, all different within a row
- prob_one: float32 [2048, 2], P('dp'), may hold values from 0.05 to 0.6
- tokens_two: bfloat16 [2048, 2048], P('dp'), may hold values from -6 to 6
- route_two: int32 [2048, 2], P('dp'), may hold values from 0 to 7, all different within a row
- prob_two: float32 [2048, 2], P('dp'), may hold values from 0.05 to 0.6
- old_order: int32 [8], replicated, may hold values from 0 to 7, each once
- new_order: int32 [8], replicated, may hold values from 0 to 7, each once
Outputs:
- moved_master: float32 [8, 3, 768, 2048], P('slot', None, 'hid', 'dp')
- moved_first: float32 [8, 3, 768, 2048], P('slot', None, 'hid', 'dp')
- moved_second: float32 [8, 3, 768, 2048], P('slot', None, 'hid', 'dp')
- next_output: bfloat16 [2048, 2048], P('dp', ('slot', 'hid'))
Inputs may be any that keep to these rules, and one draw needn't show every extreme that they name: `old_order`: lists each of the 8 experts once. `new_order`: lists each of the 8 experts once. `route_one`: each row names 2 different experts. `route_two`: each row names 2 different experts.
All inputs are finite; a program needn't handle non-finite values.
Results may differ from a plain program's by a relative error of at most 0.017.
Values may be sent and summed in bfloat16 or wider, within the bound.
A program may use at most 192 MiB of HBM per device.

v0:
```python
import jax
import jax.numpy as jnp
from jax import lax
from jax.sharding import PartitionSpec as P

learn_rate = 0.001
beta_one = 0.9
beta_two = 0.95
epsilon = 1e-08
decay_rate = 0.1


def rows_by(left, right):
    return lax.dot_general(
        left, right, (((1,), (1,)), ((), ())), preferred_element_type=jnp.float32
    )


def cols_by(left, right):
    return lax.dot_general(
        left, right, (((0,), (0,)), ((), ())), preferred_element_type=jnp.float32
    )


def expert_parts(tokens, grad_out, scaling, weights):
    gate_proj = rows_by(tokens, weights[0])
    up_proj = rows_by(tokens, weights[1])
    logistic = jax.nn.sigmoid(gate_proj)
    swish_gate = gate_proj * logistic
    activated = (swish_gate * up_proj).astype(jnp.bfloat16)
    scaled_grad = (scaling[:, None] * grad_out.astype(jnp.float32)).astype(jnp.bfloat16)
    d_activated = rows_by(scaled_grad, weights[2])
    d_gate = (d_activated * up_proj * logistic * (1.0 + gate_proj * (1.0 - logistic))).astype(
        jnp.bfloat16
    )
    d_up = (d_activated * swish_gate).astype(jnp.bfloat16)
    return (d_gate, d_up, activated, scaled_grad)


def expert_out(tokens, scaling, weights):
    gate_proj = rows_by(tokens, weights[0])
    up_proj = rows_by(tokens, weights[1])
    mixed = (scaling[:, None] * gate_proj * jax.nn.sigmoid(gate_proj) * up_proj).astype(
        jnp.bfloat16
    )
    return jnp.dot(mixed, weights[2], preferred_element_type=jnp.float32)


def adamw_update(master, moment_a, moment_b, grad_sum):
    new_a = beta_one * moment_a + (1.0 - beta_one) * grad_sum
    new_b = beta_two * moment_b + (1.0 - beta_two) * grad_sum * grad_sum
    fixed_a = new_a / (1.0 - beta_one**10)
    fixed_b = new_b / (1.0 - beta_two**10)
    new_master = master - learn_rate * (
        fixed_a / (jnp.sqrt(fixed_b) + epsilon) + decay_rate * master
    )
    return (new_master, new_a, new_b)


def coefficients(routes, probs, expert_ids):
    matches = routes[:, :, None] == expert_ids[None, None, :]
    return jnp.sum(jnp.where(matches, probs[:, :, None], 0.0), axis=1)


def per_device(
    master_weights,
    first_moment,
    second_moment,
    tokens_one,
    grad_out,
    route_one,
    prob_one,
    tokens_two,
    route_two,
    prob_two,
    old_order,
    new_order,
):
    local_count = master_weights.shape[0]
    slot_index = lax.axis_index("slot")
    offset = slot_index * local_count
    held_ids = lax.dynamic_slice_in_dim(old_order, offset, local_count)
    shard_weights = master_weights.astype(jnp.bfloat16)
    full_weights = lax.all_gather(shard_weights, "dp", axis=3, tiled=True)
    scaling_one = coefficients(route_one, prob_one, held_ids)
    parts = [
        expert_parts(tokens_one, grad_out, scaling_one[:, expert], full_weights[expert])
        for expert in range(local_count)
    ]
    gradients = jnp.stack(
        [
            jnp.stack(
                [
                    cols_by(part[0], tokens_one),
                    cols_by(part[1], tokens_one),
                    cols_by(part[2], part[3]),
                ]
            )
            for part in parts
        ]
    )
    owned_grads = lax.psum_scatter(
        gradients.astype(jnp.bfloat16), "dp", scatter_dimension=3, tiled=True
    ).astype(jnp.float32)
    new_master, new_a, new_b = adamw_update(
        master_weights, first_moment, second_moment, owned_grads
    )
    positions = jnp.arange(old_order.shape[0], dtype=jnp.int32)
    source = jnp.sum(
        jnp.where(old_order[None, :] == new_order[:, None], positions[None, :], 0), axis=1
    )
    gathered_states = (
        lax.all_gather(new_master, "slot", axis=0, tiled=True),
        lax.all_gather(new_a, "slot", axis=0, tiled=True),
        lax.all_gather(new_b, "slot", axis=0, tiled=True),
    )
    wanted = lax.dynamic_slice_in_dim(source, offset, local_count)
    moved_states = tuple((jnp.take(state_block, wanted, axis=0) for state_block in gathered_states))
    moved_master, moved_first, moved_second = moved_states
    next_shard = new_master.astype(jnp.bfloat16)
    next_full = lax.all_gather(next_shard, "dp", axis=3, tiled=True)
    scaling_two = coefficients(route_two, prob_two, held_ids)
    partial_value = expert_out(tokens_two, scaling_two[:, 0], next_full[0])
    expert = 1
    partial_value = partial_value + expert_out(
        tokens_two, scaling_two[:, expert], next_full[expert]
    )
    mixed_out = lax.psum_scatter(
        partial_value, ("slot", "hid"), scatter_dimension=1, tiled=True
    ).astype(jnp.bfloat16)
    return (moved_master, moved_first, moved_second, mixed_out)


def solution(mesh):
    in_specs = (
        P("slot", None, "hid", "dp"),
        P("slot", None, "hid", "dp"),
        P("slot", None, "hid", "dp"),
        P("dp", None),
        P("dp", None),
        P("dp", None),
        P("dp", None),
        P("dp", None),
        P("dp", None),
        P("dp", None),
        P(),
        P(),
    )
    out_specs = (
        P("slot", None, "hid", "dp"),
        P("slot", None, "hid", "dp"),
        P("slot", None, "hid", "dp"),
        P("dp", ("slot", "hid")),
    )
    return jax.shard_map(
        per_device, mesh=mesh, in_specs=in_specs, out_specs=out_specs, check_vma=False
    )
```

profile of v0, /device:TPU:0, one launch (start us, length us, event | category | flops | bytes accessed | tf_op | source)
XLA Modules:
  0.0 761.6 jit_solution(9084671307208111710)
XLA Ops:
  7.3 4.1 convert_element_type.49
  11.7 65.2 %all-gather.6.cloned.1.call-done = bf16[2,3,192,2048]{3,2,1,0:T(8,128)(2,1)} async-done(((bf16[2,3,192,1024]{3,2,1,0:T(8,128)(2,1)}), bf16[2,3,192,2048]{3,2,1,0:T(8,128)(2,1)}) %all-gather.6.cloned.1.call-update) | async-done | bytes 4718608 | tf_op jit(solution)/shard_map/all_gather | solution.py:84
  76.9 4.1 fusion.23
  81.0 4.0 fusion.14
  86.1 1.5 fusion.24
  92.7 1.6 fusion.11
  95.4 1.5 fusion.22
  100.1 2.6 pad_maximum_fusion
  102.8 60.2 %reduce-scatter.3.cloned.1.call-done = bf16[2,3,192,1024]{3,2,1,0:T(8,128)(2,1)} async-done(((bf16[2,3,192,2048]{3,2,1,0:T(8,128)(2,1)}), bf16[2,3,192,1024]{3,2,1,0:T(8,128)(2,1)}) %reduce-scatter.3.cloned.1.call-update) | async-done | bytes 2359312 | tf_op jit(solution)/shard_map/reduce_scatter | solution.py:102
  163.0 11.4 %fusion.59 = (bf16[2,3,192,1024]{3,2,1,0:T(8,128)(2,1)}, f32[2,3,192,1024]{3,2,1,0:T(8,128)}, f32[2,3,192,1024]{3,2,1,0:T(8,128)}, f32[2,3,192,1024]{3,2,1,0:T(8,128)}) fusion(f32[2,3,192,1024]{3,2,1,0:T(8,128)} %param.14, bf16[2,3,192,1024]{3,2,1,0:T(8,128)(2,1)} %reduce-scatter.3.cloned.1.call-done, f32[2,3,192,1024]{3,2,1,0:T(8,128)} %param.15, ...), kind=kLoop, calls=%fused_computation.100 | loop fusion | flops 20054016 | bytes 33030144 | tf_op jit(solution)/shard_map/convert_element_type | solution.py:120
  174.4 62.7 %all-gather.14.cloned.1.call-done = bf16[2,3,192,2048]{3,2,1,0:T(8,128)(2,1)} async-done(((bf16[2,3,192,1024]{3,2,1,0:T(8,128)(2,1)}), bf16[2,3,192,2048]{3,2,1,0:T(8,128)(2,1)}) %all-gather.14.cloned.1.call-update) | async-done | bytes 4718608 | tf_op jit(solution)/shard_map/all_gather | solution.py:121
  237.1 4.1 fusion.20
  241.3 2.7 fusion.19
  243.9 8.7 %fusion.17 = f32[1024,2048]{1,0:T(8,128)} fusion(bf16[1024,2048]{1,0:T(8,128)(2,1)} %param.21, bf16[2,3,192,2048]{3,2,1,0:T(8,128)(2,1)} %all-gather.14.cloned.1.call-done, f32[192,1024]{1,0:T(8,128)S(1)} %fusion.20, f32[1024]{0:T(1024)S(1)} %bitcast.71), kind=kOutput, calls=%fused_computation.36 | convolution fusion | flops 1611988992 | bytes 14946304 | tf_op jit(solution)/shard_map/dot_general | solution.py:46
  252.6 11.2 %convolution_add_fusion = f32[1024,2048]{1,0:T(8,128)} fusion(f32[1024,2048]{1,0:T(8,128)} %fusion.17, bf16[1024,2048]{1,0:T(8,128)(2,1)} %param.21, bf16[2,3,192,2048]{3,2,1,0:T(8,128)(2,1)} %all-gather.14.cloned.1.call-done, f32[192,1024]{1,0:T(8,128)S(1)} %fusion.19, f32[1024]{0:T(1024)S(1)} %bitcast.70), kind=kOutput, calls=%fused_computation.13 | convolution fusion | flops 1614086144 | bytes 23334912 | tf_op jit(solution)/shard_map/dot_general | solution.py:46
  266.1 101.5 %reduce-scatter.5.cloned.1.call-done = f32[1024,128]{1,0:T(8,128)} async-done(((f32[1024,2048]{1,0:T(8,128)}), f32[1024,128]{1,0:T(8,128)}) %reduce-scatter.5.cloned.1.call-update) | async-done | bytes 524304 | tf_op jit(solution)/shard_map/reduce_scatter | solution.py:128
  367.6 1.8 convert_element_type.61
  369.4 119.9 %all-gather.8.cloned.1.call-done = f32[8,3,192,1024]{3,2,1,0:T(8,128)} async-done(((f32[2,3,192,1024]{3,2,1,0:T(8,128)}), f32[8,3,192,1024]{3,2,1,0:T(8,128)}) %all-gather.8.cloned.1.call-update) | async-done | bytes 18874384 | tf_op jit(solution)/shard_map/all_gather | solution.py:113
  489.3 9.7 %gather_fusion = f32[2,3,192,1024]{3,2,1,0:T(8,128)} fusion(f32[8,3,192,1024]{3,2,1,0:T(8,128)} %all-gather.8.cloned.1.call-done, s32[1024]{0:T(1024)S(1)} %pad_clamp_fusion), kind=kCustom, calls=%fused_computation.clone | custom fusion | bytes 9437192 | tf_op jit(solution)/shard_map/jit(_take)/gather | solution.py:118
  499.0 112.4 %all-gather.10.cloned.1.call-done = f32[8,3,192,1024]{3,2,1,0:T(8,128)} async-done(((f32[2,3,192,1024]{3,2,1,0:T(8,128)}), f32[8,3,192,1024]{3,2,1,0:T(8,128)}) %all-gather.10.cloned.1.call-update) | async-done | bytes 18874384 | tf_op jit(solution)/shard_map/all_gather | solution.py:114
  611.3 9.7 %gather_fusion.1 = f32[2,3,192,1024]{3,2,1,0:T(8,128)} fusion(f32[8,3,192,1024]{3,2,1,0:T(8,128)} %all-gather.10.cloned.1.call-done, s32[1024]{0:T(1024)S(1)} %pad_clamp_fusion), kind=kCustom, calls=%fused_computation.1.clone | custom fusion | bytes 9437192 | tf_op jit(solution)/shard_map/jit(_take)/gather | solution.py:118
  621.0 112.5 %all-gather.12.cloned.1.call-done = f32[8,3,192,1024]{3,2,1,0:T(8,128)} async-done(((f32[2,3,192,1024]{3,2,1,0:T(8,128)}), f32[8,3,192,1024]{3,2,1,0:T(8,128)}) %all-gather.12.cloned.1.call-update) | async-done | bytes 18874384 | tf_op jit(solution)/shard_map/all_gather | solution.py:115
  733.5 9.4 %gather_fusion.2 = f32[2,3,192,1024]{3,2,1,0:T(8,128)} fusion(f32[8,3,192,1024]{3,2,1,0:T(8,128)} %all-gather.12.cloned.1.call-done, s32[1024]{0:T(1024)S(1)} %pad_clamp_fusion), kind=kCustom, calls=%fused_computation.2.clone | custom fusion | bytes 9437192 | tf_op jit(solution)/shard_map/jit(_take)/gather | solution.py:118
  742.9 11.9 %broadcast_select_fusion = (f32[2,3,192,1024]{3,2,1,0:T(8,128)}, f32[2,3,192,1024]{3,2,1,0:T(8,128)}, f32[2,3,192,1024]{3,2,1,0:T(8,128)}) fusion(f32[2,3,192,1024]{3,2,1,0:T(8,128)} %gather_fusion.2, pred[2]{0:T(512)(128)(4,1)S(1)} %get-tuple-element.11, f32[2,3,192,1024]{3,2,1,0:T(8,128)} %gather_fusion.1, f32[2,3,192,1024]{3,2,1,0:T(8,128)} %gather_fusion), kind=kLoop, calls=%fused_computation.28 | loop fusion | flops 3538944 | bytes 28311554 | tf_op jit(solution)/shard_map/jit(_take)/select_n | solution.py:118
  (49 shorter events, 12.8 us)
Async XLA Ops:
  7.2 4.3 copy-start.8
  7.2 4.4 copy-start.4
  7.2 4.4 copy-start.3
  7.2 4.4 copy-start.2
  7.2 4.4 copy-start.1
  7.2 69.7 %all-gather.6.cloned.1.call-start = ((), (), s32[]{:S(2)}) async-start(), calls=%async_computation.2 | async-start | bytes 7077888 | tf_op jit(solution)/shard_map/all_gather | solution.py:84
  11.4 151.6 %reduce-scatter.3.cloned.1.call-start = ((), (), s32[]{:S(2)}) async-start(), calls=%async_computation.3 | async-start | bytes 7077888 | tf_op jit(solution)/shard_map/reduce_scatter | solution.py:102
  76.9 4.1 copy-start.5
  81.0 4.1 copy-start.6
  87.7 2.2 copy-start.7
  102.7 134.4 %all-gather.14.cloned.1.call-start = ((), (), s32[]{:S(2)}) async-start(), calls=%async_computation.7 | async-start | bytes 7077888 | tf_op jit(solution)/shard_map/all_gather | solution.py:121
  174.3 193.3 %reduce-scatter.5.cloned.1.call-start = ((), (), s32[]{:S(2)}) async-start(), calls=%async_computation.8 | async-start | bytes 8912896 | tf_op jit(solution)/shard_map/reduce_scatter | solution.py:128
  237.1 4.1 copy-start
  263.9 225.4 %all-gather.8.cloned.1.call-start = ((), (), s32[]{:S(2)}) async-start(), calls=%async_computation.4 | async-start | bytes 23592960 | tf_op jit(solution)/shard_map/all_gather | solution.py:113
  264.5 346.9 %all-gather.10.cloned.1.call-start = ((), (), s32[]{:S(2)}) async-start(), calls=%async_computation.5 | async-start | bytes 23592960 | tf_op jit(solution)/shard_map/all_gather | solution.py:114
  264.5 1.3 copy-start.9
  265.1 468.5 %all-gather.12.cloned.1.call-start = ((), (), s32[]{:S(2)}) async-start(), calls=%async_computation.6 | async-start | bytes 23592960 | tf_op jit(solution)/shard_map/all_gather | solution.py:115
Sparse Core Ops, SparseCore 0:
  11.5 65.3 all-gather.5
  102.9 60.0 reduce-scatter.2
  174.5 62.6 all-gather.13
  264.0 103.5 reduce-scatter.4
  369.6 119.6 all-gather.7
  491.3 119.9 all-gather.9
  613.5 119.9 all-gather.11
where the time goes:
time: 762 us
  waiting for transfers between devices  636 us (83%)
  matrix products  48.3 us (6%)
  other arithmetic  32.6 us (4%)
  local copies, waits for them, and re-layouts  29.8 us (4%)
  between operations  14.4 us (2%)
    all_gather x1, waiting for transfers between devices, per_device(): lax.all_gather(new_master, 'slot', axis=0, tiled=True)  120 us
    all_gather x1, waiting for transfers between devices, per_device(): lax.all_gather(new_b, 'slot', axis=0, tiled=True)  113 us
    all_gather x1, waiting for transfers between devices, per_device(): lax.all_gather(new_a, 'slot', axis=0, tiled=True)  112 us
    reduce_scatter x1, waiting for transfers between devices, per_device(): lax.psum_scatter(partial_value, ('slot', 'hid'), scatter_dimension=1, til...  102 us
    all_gather x1, waiting for transfers between devices, per_device(): full_weights = lax.all_gather(shard_weights, 'dp', axis=3, tiled=True)  65.2 us
    all_gather x1, waiting for transfers between devices, per_device(): next_full = lax.all_gather(next_shard, 'dp', axis=3, tiled=True)  62.7 us
    reduce_scatter x1, waiting for transfers between devices, per_device(): lax.psum_scatter(gradients.astype(jnp.bfloat16), 'dp', scatter_dimension=...  60.2 us
    gather x3, local copies, waits for them, and re-layouts, per_device(): jnp.take(state_block, wanted, axis=0)  28.7 us
  transfers between devices with their start and end apart: 7, of which 7 were waited for; matrix products, arithmetic and copies ran while one was open for 3% of the time, Pallas kernels for 0%

commit v1 on v0

--- a/solution.py
+++ b/solution.py
@@ -8,6 +8,32 @@
 beta_two = 0.95
 epsilon = 1e-08
 decay_rate = 0.1
+
+
+def serve_the_types(x_part, axis_tag):
+    heard = jax.lax.axis_size(axis_tag)
+    block_last, step_out, mid_arr = (heard, jax.lax.axis_index(axis_tag), x_part.shape[0])
+    made = []
+    for p in [*range(block_last)]:
+        made.append((p, (p + 1) % block_last))
+    ledger = []
+    for p in tuple(range(block_last)):
+        ledger.append((p, (p - 1) % block_last))
+    seen_now = jnp.zeros((*x_part.shape[:0], block_last * mid_arr, *x_part.shape[1:]), x_part.dtype)
+    seen_now = lax.dynamic_update_slice_in_dim(seen_now, x_part, step_out * mid_arr, axis=0)
+    a_now = vec_out = x_part
+    lower = block_last // 2
+    for k in tuple(range(1, lower + 1)):
+        a_now = jax.lax.ppermute(a_now, axis_tag, made)
+        seen_now = lax.dynamic_update_slice_in_dim(
+            seen_now, a_now, (step_out - k) % block_last * mid_arr, axis=0
+        )
+        if k < block_last - lower:
+            vec_out = jax.lax.ppermute(vec_out, axis_tag, ledger)
+            seen_now = lax.dynamic_update_slice_in_dim(
+                seen_now, vec_out, (step_out + k) % block_last * mid_arr, axis=0
+            )
+    return seen_now
 
 
 def rows_by(left, right):
@@ -112,7 +138,7 @@
     gathered_states = (
         lax.all_gather(new_master, "slot", axis=0, tiled=True),
         lax.all_gather(new_a, "slot", axis=0, tiled=True),
-        lax.all_gather(new_b, "slot", axis=0, tiled=True),
+        serve_the_types(new_b, "slot"),
     )
     wanted = lax.dynamic_slice_in_dim(source, offset, local_count)
     moved_states = tuple((jnp.take(state_block, wanted, axis=0) for state_block in gathered_states))

time: 762 us -> 705 us (0.925)
  waiting for transfers between devices: 636 us -> 546 us
  local copies, waits for them, and re-layouts: 29.8 us -> 60.5 us
    ppermute x0 -> x3, waiting for transfers between devices: none -> 241 us  [the longest x2 241 us: serve_the_types(): a_now = jax.lax.ppermute(a_now, axis_tag, made)]
    all_gather x1, waiting for transfers between devices: 120 us -> 2.03 us  [per_device(): lax.all_gather(new_master, 'slot', axis=0, tiled=True)]
    all_gather x1 -> x0, waiting for transfers between devices: 113 us -> none  [per_device(): lax.all_gather(new_b, 'slot', axis=0, tiled=True)]
    reduce_scatter x1, waiting for transfers between devices: 102 us -> 0.01 us  [per_device(): lax.psum_scatter(partial_value, ('slot', 'hid'), scatter_dimension=1, til...]
    dynamic_update_slice x0 -> x4, local copies, waits for them, and re-layouts: none -> 18.1 us  [the longest x2 10.3 us: serve_the_types(): lax.dynamic_update_slice_in_dim(seen_now, a_now, (step_out - k) % block_l...]
    broadcast_in_dim x0 -> x1, local copies, waits for them, and re-layouts: none -> 13.1 us  [serve_the_types(): jnp.zeros((*x_part.shape[:0], block_last * mid_arr, *x_part.shape[1:]), x...]
  transfers between devices with their start and end apart: 7 -> 9, of which waited for: 7 -> 7; matrix products, arithmetic and copies ran while one was open for 3% -> 7% of each run, Pallas kernels for 0% -> 0%
where the time goes in v1:
time: 705 us; the launch traced here: 704 us
  waiting for transfers between devices  546 us (77%)
  local copies, waits for them, and re-layouts  60.5 us (9%)
  matrix products  48.2 us (7%)
  other arithmetic  32.6 us (5%)
  between operations  14.4 us (2%)
    ppermute x2, waiting for transfers between devices, serve_the_types(): a_now = jax.lax.ppermute(a_now, axis_tag, made)  241 us
    all_gather x1, waiting for transfers between devices, per_device(): lax.all_gather(new_a, 'slot', axis=0, tiled=True)  114 us
    all_gather x1, waiting for transfers between devices, per_device(): full_weights = lax.all_gather(shard_weights, 'dp', axis=3, tiled=True)  65.2 us
    all_gather x1, waiting for transfers between devices, per_device(): next_full = lax.all_gather(next_shard, 'dp', axis=3, tiled=True)  62.7 us
    reduce_scatter x1, waiting for transfers between devices, per_device(): lax.psum_scatter(gradients.astype(jnp.bfloat16), 'dp', scatter_dimension=...  60.2 us
    gather x3, local copies, waits for them, and re-layouts, per_device(): jnp.take(state_block, wanted, axis=0)  28.2 us
    dot_general x8, matrix products, rows_by(): lax.dot_general(left, right, (((1,), (1,)), ((), ())), preferred_element_...  21.1 us
    dot_general x2, matrix products, expert_out(): return jnp.dot(mixed, weights[2], preferred_element_type=jnp.float32)  19.9 us
  transfers between devices with their start and end apart: 9, of which 7 were waited for; matrix products, arithmetic and copies ran while one was open for 7% of the time, Pallas kernels for 0%

profile of v1, /device:TPU:0, one launch (start us, length us, event | category | flops | bytes accessed | tf_op | source)
XLA Modules:
  0.0 704.0 jit_solution(3758802639195248260)
XLA Ops:
  7.3 4.1 convert_element_type.49
  11.7 65.2 %all-gather.5.cloned.1.call-done = bf16[2,3,192,2048]{3,2,1,0:T(8,128)(2,1)} async-done(((bf16[2,3,192,1024]{3,2,1,0:T(8,128)(2,1)}), bf16[2,3,192,2048]{3,2,1,0:T(8,128)(2,1)}) %all-gather.5.cloned.1.call-update) | async-done | bytes 4718608 | tf_op jit(solution)/shard_map/all_gather | solution.py:110
  76.9 4.1 fusion.23
  81.0 4.0 fusion.14
  100.1 2.6 pad_maximum_fusion
  102.8 60.2 %reduce-scatter.3.cloned.1.call-done = bf16[2,3,192,1024]{3,2,1,0:T(8,128)(2,1)} async-done(((bf16[2,3,192,2048]{3,2,1,0:T(8,128)(2,1)}), bf16[2,3,192,1024]{3,2,1,0:T(8,128)(2,1)}) %reduce-scatter.3.cloned.1.call-update) | async-done | bytes 2359312 | tf_op jit(solution)/shard_map/reduce_scatter | solution.py:128
  163.0 11.4 %fusion.59 = (bf16[2,3,192,1024]{3,2,1,0:T(8,128)(2,1)}, f32[2,3,192,1024]{3,2,1,0:T(8,128)}, f32[2,3,192,1024]{3,2,1,0:T(8,128)}, f32[2,3,192,1024]{3,2,1,0:T(8,128)}) fusion(f32[2,3,192,1024]{3,2,1,0:T(8,128)} %param.14, bf16[2,3,192,1024]{3,2,1,0:T(8,128)(2,1)} %reduce-scatter.3.cloned.1.call-done, f32[2,3,192,1024]{3,2,1,0:T(8,128)} %param.15, ...), kind=kLoop, calls=%fused_computation.104 | loop fusion | flops 20054016 | bytes 33030144 | tf_op jit(solution)/shard_map/convert_element_type | solution.py:146
  174.4 62.7 %all-gather.11.cloned.1.call-done = bf16[2,3,192,2048]{3,2,1,0:T(8,128)(2,1)} async-done(((bf16[2,3,192,1024]{3,2,1,0:T(8,128)(2,1)}), bf16[2,3,192,2048]{3,2,1,0:T(8,128)(2,1)}) %all-gather.11.cloned.1.call-update) | async-done | bytes 4718608 | tf_op jit(solution)/shard_map/all_gather | solution.py:147
  237.1 4.1 fusion.20
  241.3 2.7 fusion.19
  243.9 8.7 %fusion.17 = f32[1024,2048]{1,0:T(8,128)} fusion(bf16[1024,2048]{1,0:T(8,128)(2,1)} %param.21, bf16[2,3,192,2048]{3,2,1,0:T(8,128)(2,1)} %all-gather.11.cloned.1.call-done, f32[192,1024]{1,0:T(8,128)S(1)} %fusion.20, f32[1024]{0:T(1024)S(1)} %bitcast.73), kind=kOutput, calls=%fused_computation.36 | convolution fusion | flops 1611988992 | bytes 14946304 | tf_op jit(solution)/shard_map/dot_general | solution.py:72
  252.6 11.2 %convolution_add_fusion = f32[1024,2048]{1,0:T(8,128)} fusion(f32[1024,2048]{1,0:T(8,128)} %fusion.17, bf16[1024,2048]{1,0:T(8,128)(2,1)} %param.21, bf16[2,3,192,2048]{3,2,1,0:T(8,128)(2,1)} %all-gather.11.cloned.1.call-done, f32[192,1024]{1,0:T(8,128)S(1)} %fusion.19, f32[1024]{0:T(1024)S(1)} %bitcast.72), kind=kOutput, calls=%fused_computation.13 | convolution fusion | flops 1614086144 | bytes 23334912 | tf_op jit(solution)/shard_map/dot_general | solution.py:72
  266.8 129.0 %collective-permute-done = f32[2,3,192,1024]{3,2,1,0:T(8,128)} collective-permute-done((f32[2,3,192,1024]{3,2,1,0:T(8,128)}, f32[2,3,192,1024]{3,2,1,0:T(8,128)}, u32[]{:S(2)}, u32[]{:S(2)}) %collective-permute-start) | collective-permute-done | bytes 4718624 | tf_op jit(solution)/shard_map/ppermute | solution.py:27
  396.1 13.1 %broadcast_in_dim.55 = f32[8,3,192,1024]{3,2,1,0:T(8,128)} broadcast(f32[]{:T(128)} %constant.56.clone.1), dimensions={} | broadcast | bytes 18874372 | tf_op jit(solution)/shard_map/broadcast_in_dim | solution.py:22
  409.2 2.5 constant_dynamic-update-slice_fusion.3
  411.7 5.2 constant_dynamic-update-slice_fusion.2
  416.9 5.3 constant_dynamic-update-slice_fusion.1
  422.2 112.4 %collective-permute-done.2 = f32[2,3,192,1024]{3,2,1,0:T(8,128)} collective-permute-done((f32[2,3,192,1024]{3,2,1,0:T(8,128)}, f32[2,3,192,1024]{3,2,1,0:T(8,128)}, u32[]{:S(2)}, u32[]{:S(2)}) %collective-permute-start.2) | collective-permute-done | bytes 4718624 | tf_op jit(solution)/shard_map/ppermute | solution.py:27
  534.6 5.1 constant_dynamic-update-slice_fusion
  539.8 9.4 %gather_fusion.2 = f32[2,3,192,1024]{3,2,1,0:T(8,128)} fusion(f32[8,3,192,1024]{3,2,1,0:T(8,128)} %constant_dynamic-update-slice_fusion, s32[1024]{0:T(1024)S(1)} %pad_clamp_fusion), kind=kCustom, calls=%fused_computation.2.clone | custom fusion | bytes 9437192 | tf_op jit(solution)/shard_map/jit(_take)/gather | solution.py:144
  553.0 9.4 %gather_fusion = f32[2,3,192,1024]{3,2,1,0:T(8,128)} fusion(f32[8,3,192,1024]{3,2,1,0:T(8,128)} %all-gather.7.cloned.1.call-done, s32[1024]{0:T(1024)S(1)} %pad_clamp_fusion), kind=kCustom, calls=%fused_computation.clone | custom fusion | bytes 9437192 | tf_op jit(solution)/shard_map/jit(_take)/gather | solution.py:144
  562.3 113.6 %all-gather.9.cloned.1.call-done = f32[8,3,192,1024]{3,2,1,0:T(8,128)} async-done(((f32[2,3,192,1024]{3,2,1,0:T(8,128)}), f32[8,3,192,1024]{3,2,1,0:T(8,128)}) %all-gather.9.cloned.1.call-update) | async-done | bytes 18874384 | tf_op jit(solution)/shard_map/all_gather | solution.py:140
  675.9 9.4 %gather_fusion.1 = f32[2,3,192,1024]{3,2,1,0:T(8,128)} fusion(f32[8,3,192,1024]{3,2,1,0:T(8,128)} %all-gather.9.cloned.1.call-done, s32[1024]{0:T(1024)S(1)} %pad_clamp_fusion), kind=kCustom, calls=%fused_computation.1.clone | custom fusion | bytes 9437192 | tf_op jit(solution)/shard_map/jit(_take)/gather | solution.py:144
  685.3 11.9 %broadcast_select_fusion = (f32[2,3,192,1024]{3,2,1,0:T(8,128)}, f32[2,3,192,1024]{3,2,1,0:T(8,128)}, f32[2,3,192,1024]{3,2,1,0:T(8,128)}) fusion(f32[2,3,192,1024]{3,2,1,0:T(8,128)} %gather_fusion.2, pred[2]{0:T(512)(128)(4,1)S(1)} %get-tuple-element.11, f32[2,3,192,1024]{3,2,1,0:T(8,128)} %gather_fusion.1, f32[2,3,192,1024]{3,2,1,0:T(8,128)} %gather_fusion), kind=kLoop, calls=%fused_computation.28 | loop fusion | flops 3538944 | bytes 28311554 | tf_op jit(solution)/shard_map/jit(_take)/select_n | solution.py:144
  (62 shorter events, 22.5 us)
Async XLA Ops:
  7.2 4.3 copy-start.8
  7.2 4.4 copy-start.4
  7.2 4.4 copy-start.3
  7.2 4.4 copy-start.2
  7.2 4.4 copy-start.1
  7.2 69.7 %all-gather.5.cloned.1.call-start = ((), (), s32[]{:S(2)}) async-start(), calls=%async_computation.2 | async-start | bytes 7077888 | tf_op jit(solution)/shard_map/all_gather | solution.py:110
  11.4 151.6 %reduce-scatter.3.cloned.1.call-start = ((), (), s32[]{:S(2)}) async-start(), calls=%async_computation.3 | async-start | bytes 7077888 | tf_op jit(solution)/shard_map/reduce_scatter | solution.py:128
  76.9 4.1 copy-start.5
  81.0 4.1 copy-start.6
  87.7 2.2 copy-start.7
  102.8 134.4 %all-gather.11.cloned.1.call-start = ((), (), s32[]{:S(2)}) async-start(), calls=%async_computation.6 | async-start | bytes 7077888 | tf_op jit(solution)/shard_map/all_gather | solution.py:147
  174.4 374.8 %reduce-scatter.5.cloned.1.call-start = ((), (), s32[]{:S(2)}) async-start(), calls=%async_computation.7 | async-start | bytes 8912896 | tf_op jit(solution)/shard_map/reduce_scatter | solution.py:154
  237.1 4.1 copy-start
  263.9 289.1 %all-gather.7.cloned.1.call-start = ((), (), s32[]{:S(2)}) async-start(), calls=%async_computation.4 | async-start | bytes 23592960 | tf_op jit(solution)/shard_map/all_gather | solution.py:139
  263.9 132.0 %copy-start.9 = (s32[8]{0:T(128)S(1)}, s32[8]{0:T(128)}, u32[]{:S(2)}) copy-start(s32[8]{0:T(128)} %param.25) | copy-start | bytes 100
  264.5 411.5 %all-gather.9.cloned.1.call-start = ((), (), s32[]{:S(2)}) async-start(), calls=%async_computation.5 | async-start | bytes 23592960 | tf_op jit(solution)/shard_map/all_gather | solution.py:140
  264.5 144.7 %slice-start = ((s8[4718592]{0:T(1024)(128)(4,1)}), s8[524288]{0:T(1024)(128)(4,1)S(1)}, s32[]{:S(2)}) async-start(s8[4718592]{0:T(1024)(128)(4,1)} %bitcast.70), calls=%async_computation.8 | async-start | bytes 1048576
  265.0 130.8 %collective-permute-start = (f32[2,3,192,1024]{3,2,1,0:T(8,128)}, f32[2,3,192,1024]{3,2,1,0:T(8,128)}, u32[]{:S(2)}, u32[]{:S(2)}) collective-permute-start(f32[2,3,192,1024]{3,2,1,0:T(8,128)} %get-tuple-element.10), channel_id=1, source_target_pairs={{0,4},{4,8},{8,12},{12,0},{1,5},{5,9},{9,13},{13,1},{2,6},{6,10},{... | collective-permute-start | bytes 14155784 | tf_op jit(solution)/shard_map/ppermute | solution.py:27
  265.1 151.8 %collective-permute-start.1 = (f32[2,3,192,1024]{3,2,1,0:T(8,128)}, f32[2,3,192,1024]{3,2,1,0:T(8,128)}, u32[]{:S(2)}, u32[]{:S(2)}) collective-permute-start(f32[2,3,192,1024]{3,2,1,0:T(8,128)} %get-tuple-element.10), channel_id=1, source_target_pairs={{0,12},{4,0},{8,4},{12,8},{1,13},{5,1},{9,5},{13,9},{2,14},{6,2},{... | collective-permute-start | bytes 14155784 | tf_op jit(solution)/shard_map/ppermute | solution.py:32
  395.8 138.8 %collective-permute-start.2 = (f32[2,3,192,1024]{3,2,1,0:T(8,128)}, f32[2,3,192,1024]{3,2,1,0:T(8,128)}, u32[]{:S(2)}, u32[]{:S(2)}) collective-permute-start(f32[2,3,192,1024]{3,2,1,0:T(8,128)} %collective-permute-done), channel_id=1, source_target_pairs={{0,4},{4,8},{8,12},{12,0},{1,5},{5,9},{9,13},{13,1},{2,6},{6,10},{... | collective-permute-start | bytes 14155784 | tf_op jit(solution)/shard_map/ppermute | solution.py:27
  396.1 13.1 %slice-start.1 = ((s8[4718592]{0:T(1024)(128)(4,1)}), s8[4194304]{0:T(1024)(128)(4,1)S(1)}, s32[]{:S(2)}) async-start(s8[4718592]{0:T(1024)(128)(4,1)} %bitcast.70), calls=%async_computation.9 | async-start | bytes 8388608
Sparse Core Ops, SparseCore 0:
  11.5 65.3 all-gather.4
  102.9 60.0 reduce-scatter.2
  174.5 62.6 all-gather.10
  264.0 126.0 reduce-scatter.4
  392.1 160.8 all-gather.6
  555.0 120.9 all-gather.8
